TPU v7x, 32 devices: a whole 2x2x4 slice. The times are simulated.
32 devices in a mesh: fsdp: 4 (over z), ctx: 2 (over x), tp: 4 (over y, core).
Axes of the slice: x: 2, y: 2, z: 4, core: 2. Of those that a mesh axis runs over, the one named last changes fastest.
Arguments:
- layer_in: bfloat16 [8, 1024, 1024], P('fsdp', ('ctx', 'tp')), may hold values from -6 to 6
- attn_gain: bfloat16 [1024], replicated, may hold values from 0.5 to 1.5
- ffn_gain: bfloat16 [1024], replicated, may hold values from 0.5 to 1.5
- query_weight: bfloat16 [1024, 1024], P(('fsdp', 'ctx'), 'tp'), may hold values from -0.1875 to 0.1875
- key_weight: bfloat16 [1024, 1024], P(('fsdp', 'ctx'), 'tp'), may hold values from -0.1875 to 0.1875
- value_weight: bfloat16 [1024, 1024], P(('fsdp', 'ctx'), 'tp'), may hold values from -0.1875 to 0.1875
- out_weight: bfloat16 [1024, 1024], P(('fsdp', 'ctx'), 'tp'), may hold values from -0.75 to 0.75
- variate_bias: float32 [2, 16], P(None, 'tp'), may hold values from -4 to 4
- gate_weight: bfloat16 [1024, 4096], P(('fsdp', 'ctx'), 'tp'), may hold values from -0.1875 to 0.1875
- up_weight: bfloat16 [1024, 4096], P(('fsdp', 'ctx'), 'tp'), may hold values from -0.1875 to 0.1875
- down_weight: bfloat16 [1024, 4096], P(('fsdp', 'ctx'), 'tp'), may hold values from -0.09375 to 0.09375
- segment_ids: int32 [8, 1024], P('fsdp'), may hold values from 0 to 15, never falling along the last dimension, each value on 1 to 512 neighbouring positions
- variate_ids: int32 [8, 1024], P('fsdp'), may hold values from 0 to 3
- time_ids: int32 [8, 1024], P('fsdp'), may hold values from 0 to 1023
- out_grad: bfloat16 [8, 1024, 1024], P('fsdp', ('ctx', 'tp')), may hold values from -6 to 6
Outputs:
- layer_out: bfloat16 [8, 1024, 1024], P('fsdp', ('ctx', 'tp'))
- in_grad: bfloat16 [8, 1024, 1024], P('fsdp', ('ctx', 'tp'))
- attn_gain_grad: float32 [1024], replicated
- ffn_gain_grad: float32 [1024], replicated
- query_grad: float32 [1024, 1024], P(('fsdp', 'ctx'), 'tp')
- key_grad: float32 [1024, 1024], P(('fsdp', 'ctx'), 'tp')
- value_grad: float32 [1024, 1024], P(('fsdp', 'ctx'), 'tp')
- out_weight_grad: float32 [1024, 1024], P(('fsdp', 'ctx'), 'tp')
- bias_grad: float32 [2, 16], P(None, 'tp')
- gate_grad: float32 [1024, 4096], P(('fsdp', 'ctx'), 'tp')
- up_grad: float32 [1024, 4096], P(('fsdp', 'ctx'), 'tp')
- down_grad: float32 [1024, 4096], P(('fsdp', 'ctx'), 'tp')
All inputs are finite; a program needn't handle non-finite values.
Results may differ from a plain program's by a relative error of at most 0.019.
Values may be sent and summed in bfloat16 or wider, within the bound.
No kernel may reach another device: no remote copies, remote signals or barrier semaphores. Data moves between devices by JAX's collectives and lax.ppermute only.
A program may use at most 128 MiB of HBM per device.

v0:
```python
import jax
import jax.numpy as jnp
from jax import lax
from jax.sharding import PartitionSpec as P

HEADS = 16
HEAD = 64
EPS = 1e-05
NEG = -1e30


def rms_norm(values, gain):
    return values * lax.rsqrt(jnp.mean(values * values, axis=-1, keepdims=True) + EPS) * gain


def rotate(values, time_rows):
    half_dim = values.shape[-1] // 2
    frequency = 10000.0 ** (-2.0 * jnp.arange(half_dim, dtype=jnp.float32) / values.shape[-1])
    angles = time_rows.astype(jnp.float32)[..., None, None] * frequency
    cosine = jnp.cos(angles)
    sine_part = jnp.sin(angles)
    first_half = values[..., :half_dim]
    second = values[..., half_dim:]
    return jnp.concatenate(
        [first_half * cosine - second * sine_part, second * cosine + first_half * sine_part],
        axis=-1,
    )


def swiglu(gate_vals, up_vals):
    return jax.nn.silu(gate_vals) * up_vals


def gather_rows(values):
    return lax.all_gather(values, "tp", axis=1, tiled=True)


def scatter_rows(values):
    return lax.psum_scatter(values, "tp", scatter_dimension=1, tiled=True)


def shards(
    layer_in,
    attn_gain,
    ffn_gain,
    query_weight,
    key_weight,
    value_weight,
    out_weight,
    variate_bias,
    gate_weight,
    up_weight,
    down_weight,
    segment_ids,
    variate_ids,
    time_ids,
    out_grad,
):
    seq_count, share, width = layer_in.shape
    span = share * lax.axis_size("tp")
    seq_length = segment_ids.shape[1]
    offset = lax.axis_index("ctx") * span
    local_heads = variate_bias.shape[1]
    proj_width = local_heads * HEAD
    row_count = seq_count * span
    block = 512
    block_starts = jnp.arange(span // block, dtype=jnp.int32) * block
    scale = HEAD ** (-0.5)
    my_times = lax.dynamic_slice_in_dim(time_ids, offset, span, 1)
    my_variates = lax.dynamic_slice_in_dim(variate_ids, offset, span, 1)
    my_segments = lax.dynamic_slice_in_dim(segment_ids, offset, span, 1)
    bias_same = variate_bias[0]
    bias_diff = variate_bias[1]
    gain_one = attn_gain.astype(jnp.float32)
    gain_two = ffn_gain.astype(jnp.float32)
    inputs = layer_in.astype(jnp.float32)
    rows_one = gather_rows(rms_norm(inputs, gain_one).astype(jnp.bfloat16)).reshape(
        row_count, width
    )
    query_full, key_full, value_full, out_full = (
        lax.all_gather(query_weight, ("fsdp", "ctx"), axis=0, tiled=True),
        lax.all_gather(key_weight, ("fsdp", "ctx"), axis=0, tiled=True),
        lax.all_gather(value_weight, ("fsdp", "ctx"), axis=0, tiled=True),
        lax.all_gather(out_weight, ("fsdp", "ctx"), axis=0, tiled=True),
    )
    queries_raw = jnp.dot(rows_one, query_full, preferred_element_type=jnp.float32).reshape(
        seq_count, span, local_heads, HEAD
    )
    keys_raw = jnp.dot(rows_one, key_full, preferred_element_type=jnp.float32).reshape(
        seq_count, span, local_heads, HEAD
    )
    queries = rotate(queries_raw, my_times).astype(jnp.bfloat16)
    keys_mine = rotate(keys_raw, my_times).astype(jnp.bfloat16).reshape(seq_count, span, proj_width)
    values_mine = (
        jnp.dot(rows_one, value_full, preferred_element_type=jnp.float32)
        .astype(jnp.bfloat16)
        .reshape(seq_count, span, proj_width)
    )
    keys_all, values_all = (
        lax.all_gather(keys_mine, "ctx", axis=1, tiled=True),
        lax.all_gather(values_mine, "ctx", axis=1, tiled=True),
    )

    def scores_of(query_block, key_rows, query_var, key_var, query_seg, key_seg):
        raw = (
            jnp.einsum("qhd,khd->hqk", query_block, key_rows, preferred_element_type=jnp.float32)
            * scale
        )
        same = (query_var[:, None] == key_var[None, :])[None]
        raw = raw + jnp.where(same, bias_same[:, None, None], bias_diff[:, None, None])
        return (jnp.where((query_seg[:, None] == key_seg[None, :])[None], raw, NEG), same)

    mixed_parts = []
    lse_parts = []
    for seq in range(seq_count):
        key_rows = keys_all[seq].reshape(seq_length, local_heads, HEAD)
        value_rows = values_all[seq].reshape(seq_length, local_heads, HEAD)

        def forward_block(first, seq=seq, key_rows=key_rows, value_rows=value_rows):
            query_block = queries[seq]
            query_var = my_variates[seq]
            query_seg = my_segments[seq]
            scores, same = scores_of(
                query_block, key_rows, query_var, variate_ids[seq], query_seg, segment_ids[seq]
            )
            top = jnp.max(scores, axis=-1, keepdims=True)
            expo = jnp.exp(scores - top)
            total = jnp.sum(expo, axis=-1, keepdims=True)
            probs = (expo / total).astype(jnp.bfloat16)
            mixed_block = jnp.einsum(
                "hqk,khd->qhd", probs, value_rows, preferred_element_type=jnp.float32
            )
            return (
                mixed_block.astype(jnp.bfloat16).reshape(block, proj_width),
                top[..., 0] + jnp.log(total[..., 0]),
            )

        mixed_seq, lse_seq = lax.map(forward_block, block_starts)
        mixed_parts.append(mixed_seq.reshape(span, proj_width))
        lse_parts.append(lse_seq)
    mixed = jnp.stack(mixed_parts).reshape(row_count, proj_width)
    attn_part = jnp.einsum("rp,dp->rd", mixed, out_full, preferred_element_type=jnp.float32)
    hidden = inputs + scatter_rows(attn_part.reshape(seq_count, span, width))
    rows_two = gather_rows(rms_norm(hidden, gain_two).astype(jnp.bfloat16)).reshape(
        row_count, width
    )
    gate_full, up_full, down_full = (
        lax.all_gather(gate_weight, ("fsdp", "ctx"), axis=0, tiled=True),
        lax.all_gather(up_weight, ("fsdp", "ctx"), axis=0, tiled=True),
        lax.all_gather(down_weight, ("fsdp", "ctx"), axis=0, tiled=True),
    )
    gate = jnp.dot(rows_two, gate_full, preferred_element_type=jnp.float32)
    up_vals = jnp.dot(rows_two, up_full, preferred_element_type=jnp.float32)
    act = swiglu(gate, up_vals).astype(jnp.bfloat16)
    ffn_part = jnp.einsum("rf,df->rd", act, down_full, preferred_element_type=jnp.float32)
    layer_out = (hidden + scatter_rows(ffn_part.reshape(seq_count, span, width))).astype(
        jnp.bfloat16
    )
    query_back, key_back, value_back, out_back = (
        lax.all_gather(query_weight, ("fsdp", "ctx"), axis=0, tiled=True),
        lax.all_gather(key_weight, ("fsdp", "ctx"), axis=0, tiled=True),
        lax.all_gather(value_weight, ("fsdp", "ctx"), axis=0, tiled=True),
        lax.all_gather(out_weight, ("fsdp", "ctx"), axis=0, tiled=True),
    )
    gate_back, up_back, down_back = (
        lax.all_gather(gate_weight, ("fsdp", "ctx"), axis=0, tiled=True),
        lax.all_gather(up_weight, ("fsdp", "ctx"), axis=0, tiled=True),
        lax.all_gather(down_weight, ("fsdp", "ctx"), axis=0, tiled=True),
    )
    grad_rows = gather_rows(out_grad).reshape(row_count, width)
    d_act = jnp.dot(grad_rows, down_back, preferred_element_type=jnp.float32)
    down_local = jnp.einsum("rd,rf->df", grad_rows, act, preferred_element_type=jnp.float32)
    swiglu_pull = jax.vjp(swiglu, gate, up_vals)[1]
    d_gate, d_up = swiglu_pull(d_act)
    d_gate = d_gate.astype(jnp.bfloat16)
    d_up = d_up.astype(jnp.bfloat16)
    gate_local = jnp.einsum("rd,rf->df", rows_two, d_gate, preferred_element_type=jnp.float32)
    up_local = jnp.einsum("rd,rf->df", rows_two, d_up, preferred_element_type=jnp.float32)
    d_normed_two = jnp.einsum("rf,df->rd", d_gate, gate_back, preferred_element_type=jnp.float32)
    d_normed_two = d_normed_two + jnp.einsum(
        "rf,df->rd", d_up, up_back, preferred_element_type=jnp.float32
    )
    norm_two_pull = jax.vjp(rms_norm, hidden, gain_two)[1]
    d_hidden_norm, d_gain_two = norm_two_pull(
        scatter_rows(d_normed_two.reshape(seq_count, span, width))
    )
    d_hidden = out_grad.astype(jnp.float32) + d_hidden_norm
    branch_rows = gather_rows(d_hidden.astype(jnp.bfloat16)).reshape(row_count, width)
    out_local = jnp.einsum("rd,rp->dp", branch_rows, mixed, preferred_element_type=jnp.float32)
    d_mixed = jnp.dot(branch_rows, out_back, preferred_element_type=jnp.float32).astype(
        jnp.bfloat16
    )
    d_mixed = d_mixed.reshape(seq_count, span, local_heads, HEAD)
    d_query_parts = []
    d_key_parts = []
    d_value_parts = []
    d_bias = jnp.zeros((2, local_heads), jnp.float32)
    for seq in range(seq_count):
        key_rows = keys_all[seq].reshape(seq_length, local_heads, HEAD)
        value_rows = values_all[seq].reshape(seq_length, local_heads, HEAD)

        def back_block(carry, item, seq=seq, key_rows=key_rows, value_rows=value_rows):
            d_keys, d_values, bias_sum = carry
            first, lse_block = item
            query_block = queries[seq]
            query_var = my_variates[seq]
            query_seg = my_segments[seq]
            scores, same = scores_of(
                query_block, key_rows, query_var, variate_ids[seq], query_seg, segment_ids[seq]
            )
            probs = jnp.exp(scores - lse_block[:, :, None])
            probs_low = probs.astype(jnp.bfloat16)
            d_out = d_mixed[seq]
            d_probs = jnp.einsum(
                "qhd,khd->hqk", d_out, value_rows, preferred_element_type=jnp.float32
            )
            delta = jnp.sum(probs * d_probs, axis=-1, keepdims=True)
            d_scores = (probs * (d_probs - delta)).astype(jnp.bfloat16)
            d_query = (
                jnp.einsum("hqk,khd->qhd", d_scores, key_rows, preferred_element_type=jnp.float32)
                * scale
            )
            d_keys = (
                d_keys
                + jnp.einsum(
                    "hqk,qhd->khd", d_scores, query_block, preferred_element_type=jnp.float32
                )
                * scale
            )
            d_values = d_values + jnp.einsum(
                "hqk,qhd->khd", probs_low, d_out, preferred_element_type=jnp.float32
            )
            wide_scores = d_scores.astype(jnp.float32)
            same_sum = jnp.sum(jnp.where(same, wide_scores, 0.0), axis=(1, 2))
            diff_sum = jnp.sum(jnp.where(same, 0.0, wide_scores), axis=(1, 2))
            return ((d_keys, d_values, bias_sum + jnp.stack([same_sum, diff_sum])), d_query)

        zero_rows = jnp.zeros((seq_length, local_heads, HEAD), jnp.float32)
        (d_keys, d_values, bias_sum), d_query_blocks = lax.scan(
            back_block,
            (zero_rows, zero_rows, jnp.zeros((2, local_heads), jnp.float32)),
            (block_starts, lse_parts[seq]),
        )
        d_query_parts.append(d_query_blocks.reshape(span, local_heads, HEAD))
        d_key_parts.append(d_keys.reshape(seq_length, proj_width))
        d_value_parts.append(d_values.reshape(seq_length, proj_width))
        d_bias = d_bias + bias_sum
    d_keys_mine, d_values_mine = (
        lax.psum_scatter(
            jnp.stack(d_key_parts).astype(jnp.bfloat16), "ctx", scatter_dimension=1, tiled=True
        ).astype(jnp.float32),
        lax.psum_scatter(
            jnp.stack(d_value_parts).astype(jnp.bfloat16), "ctx", scatter_dimension=1, tiled=True
        ).astype(jnp.float32),
    )

    def rope_local(values):
        return rotate(values, my_times)

    rope_pull = jax.vjp(rope_local, queries_raw)[1]
    d_query_raw = (
        rope_pull(jnp.stack(d_query_parts))[0].astype(jnp.bfloat16).reshape(row_count, proj_width)
    )
    d_key_raw = (
        rope_pull(d_keys_mine.reshape(seq_count, span, local_heads, HEAD))[0]
        .astype(jnp.bfloat16)
        .reshape(row_count, proj_width)
    )
    d_value_low = d_values_mine.astype(jnp.bfloat16).reshape(row_count, proj_width)
    query_local = jnp.einsum("rd,rp->dp", rows_one, d_query_raw, preferred_element_type=jnp.float32)
    key_local = jnp.einsum("rd,rp->dp", rows_one, d_key_raw, preferred_element_type=jnp.float32)
    value_local = jnp.einsum("rd,rp->dp", rows_one, d_value_low, preferred_element_type=jnp.float32)
    d_normed_one = jnp.einsum(
        "rp,dp->rd", d_query_raw, query_back, preferred_element_type=jnp.float32
    )
    d_normed_one = d_normed_one + jnp.einsum(
        "rp,dp->rd", d_key_raw, key_back, preferred_element_type=jnp.float32
    )
    d_normed_one = d_normed_one + jnp.einsum(
        "rp,dp->rd", d_value_low, value_back, preferred_element_type=jnp.float32
    )
    norm_one_pull = jax.vjp(rms_norm, inputs, gain_one)[1]
    d_input_norm, d_gain_one = norm_one_pull(
        scatter_rows(d_normed_one.reshape(seq_count, span, width))
    )
    in_grad = (d_hidden + d_input_norm).astype(jnp.bfloat16)
    query_grad, key_grad, value_grad, out_weight_grad = (
        lax.psum_scatter(
            query_local.astype(jnp.bfloat16), ("fsdp", "ctx"), scatter_dimension=0, tiled=True
        ).astype(jnp.float32),
        lax.psum_scatter(
            key_local.astype(jnp.bfloat16), ("fsdp", "ctx"), scatter_dimension=0, tiled=True
        ).astype(jnp.float32),
        lax.psum_scatter(
            value_local.astype(jnp.bfloat16), ("fsdp", "ctx"), scatter_dimension=0, tiled=True
        ).astype(jnp.float32),
        lax.psum_scatter(
            out_local.astype(jnp.bfloat16), ("fsdp", "ctx"), scatter_dimension=0, tiled=True
        ).astype(jnp.float32),
    )
    gate_grad, up_grad, down_grad = (
        lax.psum_scatter(
            gate_local.astype(jnp.bfloat16), ("fsdp", "ctx"), scatter_dimension=0, tiled=True
        ).astype(jnp.float32),
        lax.psum_scatter(
            up_local.astype(jnp.bfloat16), ("fsdp", "ctx"), scatter_dimension=0, tiled=True
        ).astype(jnp.float32),
        lax.psum_scatter(
            down_local.astype(jnp.bfloat16), ("fsdp", "ctx"), scatter_dimension=0, tiled=True
        ).astype(jnp.float32),
    )
    head_offset = lax.axis_index("tp") * local_heads
    bias_full = lax.dynamic_update_slice_in_dim(
        jnp.zeros((2, HEADS), jnp.float32), d_bias, head_offset, 1
    )
    attn_gain_grad, ffn_gain_grad, bias_total = lax.psum(
        (d_gain_one, d_gain_two, bias_full), ("fsdp", "ctx", "tp")
    )
    bias_grad = lax.dynamic_slice_in_dim(bias_total, head_offset, local_heads, 1)
    return (
        layer_out,
        in_grad,
        attn_gain_grad,
        ffn_gain_grad,
        query_grad,
        key_grad,
        value_grad,
        out_weight_grad,
        bias_grad,
        gate_grad,
        up_grad,
        down_grad,
    )


def solution(mesh):
    in_specs = (
        P("fsdp", ("ctx", "tp"), None),
        P(),
        P(),
        P(("fsdp", "ctx"), "tp"),
        P(("fsdp", "ctx"), "tp"),
        P(("fsdp", "ctx"), "tp"),
        P(("fsdp", "ctx"), "tp"),
        P(None, "tp"),
        P(("fsdp", "ctx"), "tp"),
        P(("fsdp", "ctx"), "tp"),
        P(("fsdp", "ctx"), "tp"),
        P("fsdp", None),
        P("fsdp", None),
        P("fsdp", None),
        P("fsdp", ("ctx", "tp"), None),
    )
    out_specs = (
        P("fsdp", ("ctx", "tp"), None),
        P("fsdp", ("ctx", "tp"), None),
        P(),
        P(),
        P(("fsdp", "ctx"), "tp"),
        P(("fsdp", "ctx"), "tp"),
        P(("fsdp", "ctx"), "tp"),
        P(("fsdp", "ctx"), "tp"),
        P(None, "tp"),
        P(("fsdp", "ctx"), "tp"),
        P(("fsdp", "ctx"), "tp"),
        P(("fsdp", "ctx"), "tp"),
    )
    return jax.shard_map(shards, mesh=mesh, in_specs=in_specs, out_specs=out_specs, check_vma=False)
```

profile of v0, /device:TPU:0, one launch (start us, length us, event | category | flops | bytes accessed | tf_op | source)
XLA Modules:
  0.0 1151.3 jit_solution(9747962312075755871)
XLA Ops:
  15.6 33.3 %all_gather.49 = bf16[1024,256]{1,0:T(8,128)(2,1)S(1)} all-gather(bf16[128,256]{1,0:T(8,128)(2,1)} %param.18), channel_id=1, replica_groups=mesh['fsdp'=4,'ctx'=2,'tp'=4] {'fsdp','ctx'}, dimensions={0}, use_global_device_ids=true | all-gather | bytes 589824 | tf_op jit(solution)/shard_map/all_gather | solution.py:81
  48.9 31.6 %all_gather.50 = bf16[1024,256]{1,0:T(8,128)(2,1)S(1)} all-gather(bf16[128,256]{1,0:T(8,128)(2,1)} %param.19), channel_id=1, replica_groups=mesh['fsdp'=4,'ctx'=2,'tp'=4] {'fsdp','ctx'}, dimensions={0}, use_global_device_ids=true | all-gather | bytes 589824 | tf_op jit(solution)/shard_map/all_gather | solution.py:82
  80.5 31.9 %all_gather.47 = bf16[1024,256]{1,0:T(8,128)(2,1)S(1)} all-gather(bf16[128,256]{1,0:T(8,128)(2,1)} %param.20), channel_id=1, replica_groups=mesh['fsdp'=4,'ctx'=2,'tp'=4] {'fsdp','ctx'}, dimensions={0}, use_global_device_ids=true | all-gather | bytes 589824 | tf_op jit(solution)/shard_map/all_gather | solution.py:83
  112.3 31.6 %all_gather.52 = bf16[1024,256]{1,0:T(8,128)(2,1)S(1)} all-gather(bf16[128,256]{1,0:T(8,128)(2,1)} %param.21), channel_id=1, replica_groups=mesh['fsdp'=4,'ctx'=2,'tp'=4] {'fsdp','ctx'}, dimensions={0}, use_global_device_ids=true | all-gather | bytes 589824 | tf_op jit(solution)/shard_map/all_gather | solution.py:84
  156.3 14.2 %all-gather.12.cloned.1.call-done = bf16[2,1024,256]{2,1,0:T(8,128)(2,1)} async-done(((bf16[2,512,256]{2,1,0:T(8,128)(2,1)}), bf16[2,1024,256]{2,1,0:T(8,128)(2,1)}) %all-gather.12.cloned.1.call-update) | async-done | bytes 1048592 | tf_op jit(solution)/shard_map/all_gather | solution.py:101
  176.9 17.1 %all-gather.14.cloned.1.call-done = bf16[2,1024,256]{1,2,0:T(8,128)(2,1)} async-done(((bf16[2,512,256]{1,2,0:T(8,128)(2,1)}), bf16[2,1024,256]{1,2,0:T(8,128)(2,1)}) %all-gather.14.cloned.1.call-update) | async-done | bytes 1048592 | tf_op jit(solution)/shard_map/all_gather | solution.py:100
  221.1 43.6 %reduce-scatter.16.cloned.1.call-done = f32[2,128,1024]{2,1,0:T(8,128)} async-done(((f32[2,512,1024]{2,1,0:T(8,128)}), f32[2,128,1024]{2,1,0:T(8,128)}) %reduce-scatter.16.cloned.1.call-update) | async-done | bytes 1048592 | tf_op jit(solution)/shard_map/reduce_scatter | solution.py:39
  272.2 23.0 %all-gather.16.cloned.1.call-done = bf16[2,512,1024]{2,1,0:T(8,128)(2,1)} async-done(((bf16[2,128,1024]{2,1,0:T(8,128)(2,1)}), bf16[2,512,1024]{2,1,0:T(8,128)(2,1)}) %all-gather.16.cloned.1.call-update) | async-done | bytes 2097168 | tf_op jit(solution)/shard_map/all_gather | solution.py:35
  301.8 45.0 %all-gather.18.cloned.1.call-done = bf16[1024,1024]{1,0:T(8,128)(2,1)} async-done(((bf16[128,1024]{1,0:T(8,128)(2,1)}), bf16[1024,1024]{1,0:T(8,128)(2,1)}) %all-gather.18.cloned.1.call-update) | async-done | bytes 2097168 | tf_op jit(solution)/shard_map/all_gather | solution.py:148
  353.4 16.1 %all-gather.24.cloned.1.call-done = bf16[2,512,1024]{2,1,0:T(8,128)(2,1)} async-done(((bf16[2,128,1024]{2,1,0:T(8,128)(2,1)}), bf16[2,512,1024]{2,1,0:T(8,128)(2,1)}) %all-gather.24.cloned.1.call-update) | async-done | bytes 2097168 | tf_op jit(solution)/shard_map/all_gather | solution.py:35
  369.5 51.7 %all-gather.22.cloned.1.call-done = bf16[1024,1024]{1,0:T(8,128)(2,1)} async-done(((bf16[128,1024]{1,0:T(8,128)(2,1)}), bf16[1024,1024]{1,0:T(8,128)(2,1)}) %all-gather.22.cloned.1.call-update) | async-done | bytes 2097168 | tf_op jit(solution)/shard_map/all_gather | solution.py:150
  421.2 9.9 multiply_convert_fusion.2
  438.7 43.1 %reduce-scatter.20.cloned.1.call-done = f32[2,128,1024]{2,1,0:T(8,128)} async-done(((f32[2,512,1024]{2,1,0:T(8,128)}), f32[2,128,1024]{2,1,0:T(8,128)}) %reduce-scatter.20.cloned.1.call-update) | async-done | bytes 1048592 | tf_op jit(solution)/shard_map/reduce_scatter | solution.py:39
  486.5 22.2 %all-gather.26.cloned.1.call-done = bf16[2,512,1024]{2,1,0:T(8,128)(2,1)} async-done(((bf16[2,128,1024]{2,1,0:T(8,128)(2,1)}), bf16[2,512,1024]{2,1,0:T(8,128)(2,1)}) %all-gather.26.cloned.1.call-update) | async-done | bytes 2097168 | tf_op jit(solution)/shard_map/all_gather | solution.py:35
  533.1 8.7 fusion
  618.3 29.3 %reduce-scatter.40.cloned.1.call-done = bf16[128,1024]{1,0:T(8,128)(2,1)} async-done(((bf16[1024,1024]{1,0:T(8,128)(2,1)}), bf16[128,1024]{1,0:T(8,128)(2,1)}) %reduce-scatter.40.cloned.1.call-update) | async-done | bytes 262160
  649.6 68.4 %reduce-scatter.38.cloned.1.call-done = bf16[128,1024]{1,0:T(8,128)(2,1)} async-done(((bf16[1024,1024]{1,0:T(8,128)(2,1)}), bf16[128,1024]{1,0:T(8,128)(2,1)}) %reduce-scatter.38.cloned.1.call-update) | async-done | bytes 262160 | tf_op jit(solution)/shard_map/reduce_scatter | solution.py:305
  719.8 68.3 %reduce-scatter.36.cloned.1.call-done = bf16[128,1024]{1,0:T(8,128)(2,1)} async-done(((bf16[1024,1024]{1,0:T(8,128)(2,1)}), bf16[128,1024]{1,0:T(8,128)(2,1)}) %reduce-scatter.36.cloned.1.call-update) | async-done | bytes 262160 | tf_op jit(solution)/shard_map/reduce_scatter | solution.py:302
  790.1 62.4 %reduce-scatter.34.cloned.1.call-done = bf16[128,256]{1,0:T(8,128)(2,1)} async-done(((bf16[1024,256]{1,0:T(8,128)(2,1)}), bf16[128,256]{1,0:T(8,128)(2,1)}) %reduce-scatter.34.cloned.1.call-update) | async-done | bytes 65552 | tf_op jit(solution)/shard_map/reduce_scatter | solution.py:297
  854.0 63.0 %reduce-scatter.32.cloned.1.call-done = bf16[128,256]{1,0:T(8,128)(2,1)} async-done(((bf16[1024,256]{1,0:T(8,128)(2,1)}), bf16[128,256]{1,0:T(8,128)(2,1)}) %reduce-scatter.32.cloned.1.call-update) | async-done | bytes 65552 | tf_op jit(solution)/shard_map/reduce_scatter | solution.py:294
  918.5 63.3 %reduce-scatter.30.cloned.1.call-done = bf16[128,256]{1,0:T(8,128)(2,1)} async-done(((bf16[1024,256]{1,0:T(8,128)(2,1)}), bf16[128,256]{1,0:T(8,128)(2,1)}) %reduce-scatter.30.cloned.1.call-update) | async-done | bytes 65552 | tf_op jit(solution)/shard_map/reduce_scatter | solution.py:291
  983.4 63.6 %reduce-scatter.28.cloned.1.call-done = bf16[128,256]{1,0:T(8,128)(2,1)} async-done(((bf16[1024,256]{1,0:T(8,128)(2,1)}), bf16[128,256]{1,0:T(8,128)(2,1)}) %reduce-scatter.28.cloned.1.call-update) | async-done | bytes 65552 | tf_op jit(solution)/shard_map/reduce_scatter | solution.py:288
  1048.4 44.4 %reduce-scatter.26.cloned.1.call-done = f32[2,128,1024]{2,1,0:T(8,128)} async-done(((f32[2,512,1024]{2,1,0:T(8,128)}), f32[2,128,1024]{2,1,0:T(8,128)}) %reduce-scatter.26.cloned.1.call-update) | async-done | bytes 1048592 | tf_op jit(solution)/shard_map/reduce_scatter | solution.py:39
  1094.4 39.8 %all-reduce.4 = (f32[1024]{0:T(1024)}, f32[1024]{0:T(1024)}, f32[2,16]{1,0:T(2,128)S(1)}) all-reduce(f32[1024]{0:T(1024)S(1)} %get-tuple-element.206, f32[1024]{0:T(1024)S(1)} %copy-done.44, f32[2,16]{1,0:T(2,128)S(1)} %dynamic_update_slice.18), channel_id=1, replica_groups=mesh['fsdp'=4,'ctx'=2,'tp'=4] {'fsdp','ctx','tp'}, use_global_device_ids=true, to_apply=%region_17.18 | all-reduce | flops 2080 | bytes 16640 | tf_op jit(solution)/shard_map/psum | solution.py:316
  (283 shorter events, 208.7 us)
Async XLA Ops:
  8.0 136.9 %all-gather.10.cloned.1.call-start = ((), (), s32[]{:S(2)}) async-start(), calls=%async_computation.13 | async-start | bytes 2621440 | tf_op jit(solution)/shard_map/all_gather | solution.py:35
  13.2 157.4 %all-gather.12.cloned.1.call-start = ((), (), s32[]{:S(2)}) async-start(), calls=%async_computation.14 | async-start | bytes 1572864 | tf_op jit(solution)/shard_map/all_gather | solution.py:101
  148.2 45.8 %all-gather.14.cloned.1.call-start = ((), (), s32[]{:S(2)}) async-start(), calls=%async_computation.15 | async-start | bytes 1572864 | tf_op jit(solution)/shard_map/all_gather | solution.py:100
  153.4 111.4 %reduce-scatter.16.cloned.1.call-start = ((), (), s32[]{:S(2)}) async-start(), calls=%async_computation.16 | async-start | bytes 5242880 | tf_op jit(solution)/shard_map/reduce_scatter | solution.py:39
  220.0 52.2 %all-gather.20.cloned.1.call-start = ((), (), s32[]{:S(2)}) async-start(), calls=%async_computation.19 | async-start | bytes 2359296 | tf_op jit(solution)/shard_map/all_gather | solution.py:149
  220.6 74.7 %all-gather.16.cloned.1.call-start = ((), (), s32[]{:S(2)}) async-start(), calls=%async_computation.17 | async-start | bytes 2621440 | tf_op jit(solution)/shard_map/all_gather | solution.py:35
  267.2 79.7 %all-gather.18.cloned.1.call-start = ((), (), s32[]{:S(2)}) async-start(), calls=%async_computation.18 | async-start | bytes 2359296 | tf_op jit(solution)/shard_map/all_gather | solution.py:148
  267.8 101.7 %all-gather.24.cloned.1.call-start = ((), (), s32[]{:S(2)}) async-start(), calls=%async_computation.22 | async-start | bytes 2621440 | tf_op jit(solution)/shard_map/all_gather | solution.py:35
  268.5 152.7 %all-gather.22.cloned.1.call-start = ((), (), s32[]{:S(2)}) async-start(), calls=%async_computation.20 | async-start | bytes 2359296 | tf_op jit(solution)/shard_map/all_gather | solution.py:150
  269.3 212.5 %reduce-scatter.20.cloned.1.call-start = ((), (), s32[]{:S(2)}) async-start(), calls=%async_computation.23 | async-start | bytes 5242880 | tf_op jit(solution)/shard_map/reduce_scatter | solution.py:39
  438.6 70.1 %all-gather.26.cloned.1.call-start = ((), (), s32[]{:S(2)}) async-start(), calls=%async_computation.24 | async-start | bytes 2621440 | tf_op jit(solution)/shard_map/all_gather | solution.py:35
  486.2 98.6 %reduce-scatter.24.cloned.1.call-start = ((), (), s32[]{:S(2)}) async-start(), calls=%async_computation.26 | async-start | bytes 1572864 | tf_op jit(solution)/shard_map/reduce_scatter | solution.py:252
  533.0 59.9 %reduce-scatter.22.cloned.1.call-start = ((), (), s32[]{:S(2)}) async-start(), calls=%async_computation.25 | async-start | bytes 1572864 | tf_op jit(solution)/shard_map/reduce_scatter | solution.py:249
  554.6 93.0 %reduce-scatter.40.cloned.1.call-start = ((), (), s32[]{:S(2)}) async-start(), calls=%async_computation.34 | async-start | bytes 2359296
  564.9 153.1 %reduce-scatter.38.cloned.1.call-start = ((), (), s32[]{:S(2)}) async-start(), calls=%async_computation.33 | async-start | bytes 2359296 | tf_op jit(solution)/shard_map/reduce_scatter | solution.py:305
  570.9 217.2 %reduce-scatter.36.cloned.1.call-start = ((), (), s32[]{:S(2)}) async-start(), calls=%async_computation.32 | async-start | bytes 2359296 | tf_op jit(solution)/shard_map/reduce_scatter | solution.py:302
  576.9 275.5 %reduce-scatter.34.cloned.1.call-start = ((), (), s32[]{:S(2)}) async-start(), calls=%async_computation.31 | async-start | bytes 589824 | tf_op jit(solution)/shard_map/reduce_scatter | solution.py:297
  580.2 336.8 %reduce-scatter.32.cloned.1.call-start = ((), (), s32[]{:S(2)}) async-start(), calls=%async_computation.30 | async-start | bytes 589824 | tf_op jit(solution)/shard_map/reduce_scatter | solution.py:294
  588.0 393.8 %reduce-scatter.30.cloned.1.call-start = ((), (), s32[]{:S(2)}) async-start(), calls=%async_computation.29 | async-start | bytes 589824 | tf_op jit(solution)/shard_map/reduce_scatter | solution.py:291
  600.0 447.0 %reduce-scatter.28.cloned.1.call-start = ((), (), s32[]{:S(2)}) async-start(), calls=%async_computation.28 | async-start | bytes 589824 | tf_op jit(solution)/shard_map/reduce_scatter | solution.py:288
  605.9 486.9 %reduce-scatter.26.cloned.1.call-start = ((), (), s32[]{:S(2)}) async-start(), calls=%async_computation.27 | async-start | bytes 5242880 | tf_op jit(solution)/shard_map/reduce_scatter | solution.py:39
  611.5 529.1 %reduce-scatter.18.cloned.1.call-start = ((), (), s32[]{:S(2)}) async-start(), calls=%async_computation.21 | async-start | bytes 5242880 | tf_op jit(solution)/shard_map/reduce_scatter | solution.py:39
  618.2 522.4 %copy-start.5 = (f32[2,128,1024]{2,1,0:T(8,128)S(1)}, f32[2,128,1024]{2,1,0:T(8,128)}, u32[]{:S(2)}) copy-start(f32[2,128,1024]{2,1,0:T(8,128)} %reduce-scatter.20.cloned.1.call-done) | copy-start | bytes 3145732
  618.3 522.4 %copy-start.32 = (f32[1024]{0:T(1024)S(1)}, f32[1024]{0:T(1024)}, u32[]{:S(2)}) copy-start(f32[1024]{0:T(1024)} %copy-done.31) | copy-start | bytes 12292
  (65 other events, 4732.4 us)
Sparse Core Ops, SparseCore 0:
  13.3 25.2 all-gather.9
  148.3 22.1 all-gather.11
  172.7 21.2 all-gather.13
  220.1 44.5 reduce-scatter.15
  438.7 42.9 reduce-scatter.19
  533.1 20.3 reduce-scatter.23
  555.8 20.3 reduce-scatter.21
  579.7 67.8 reduce-scatter.39
  651.1 66.8 reduce-scatter.37
  721.4 66.6 reduce-scatter.35
  791.5 60.9 reduce-scatter.33
  856.0 60.9 reduce-scatter.31
  920.9 60.8 reduce-scatter.29
  986.0 60.9 reduce-scatter.27
  1049.3 43.4 reduce-scatter.25
  1095.4 45.2 reduce-scatter.17
Sparse Core Ops, SparseCore 1:
  222.9 49.3 all-gather.19
  274.3 20.9 all-gather.15
  297.5 49.3 all-gather.17
  348.5 20.9 all-gather.23
  371.8 49.3 all-gather.21
  486.3 22.4 all-gather.25
where the time goes:
time: 1160 us; the launch traced here: 1150 us
  waiting for transfers between devices  750 us (65%)
  blocking collectives  168 us (14%)
  matrix products  124 us (11%)
  other arithmetic  56.5 us (5%)
  local copies, waits for them, and re-layouts  33 us (3%)
  between operations  16.9 us (1%)
    reduce_scatter x4, waiting for transfers between devices, scatter_rows(): return lax.psum_scatter(values, 'tp', scatter_dimension=1, tiled=True)  137 us
    reduce_scatter x1, waiting for transfers between devices, shards(): lax.psum_scatter(up_local.astype(jnp.bfloat16), ('fsdp', 'ctx'), scatter_...  68.4 us
    reduce_scatter x1, waiting for transfers between devices, shards(): lax.psum_scatter(gate_local.astype(jnp.bfloat16), ('fsdp', 'ctx'), scatte...  68.3 us
    reduce_scatter x1, waiting for transfers between devices, shards(): lax.psum_scatter(query_local.astype(jnp.bfloat16), ('fsdp', 'ctx'), scatt...  63.6 us
    reduce_scatter x1, waiting for transfers between devices, shards(): lax.psum_scatter(key_local.astype(jnp.bfloat16), ('fsdp', 'ctx'), scatter...  63.3 us
    reduce_scatter x1, waiting for transfers between devices, shards(): lax.psum_scatter(value_local.astype(jnp.bfloat16), ('fsdp', 'ctx'), scatt...  63 us
    reduce_scatter x1, waiting for transfers between devices, shards(): lax.psum_scatter(out_local.astype(jnp.bfloat16), ('fsdp', 'ctx'), scatter...  62.4 us
    all_gather x4, waiting for transfers between devices, gather_rows(): return lax.all_gather(values, 'tp', axis=1, tiled=True)  61.4 us
  transfers between devices with their start and end apart: 22, of which 19 were waited for; matrix products, arithmetic and copies ran while one was open for 11% of the time, Pallas kernels for 0%

commit v1 on v0

--- a/solution.py
+++ b/solution.py
@@ -7,6 +7,24 @@
 HEAD = 64
 EPS = 1e-05
 NEG = -1e30
+
+
+def gather_around(value, axis, dim):
+    ways, here, step = (lax.axis_size(axis), lax.axis_index(axis), value.shape[dim])
+    shape = [n * ways if d == dim else n for d, n in enumerate(value.shape)]
+    full = lax.dynamic_update_slice_in_dim(
+        jnp.zeros(shape, value.dtype), value, here * step, axis=dim
+    )
+    going_up = going_down = value
+    for far in range(1, ways // 2 + 1):
+        going_up = lax.ppermute(going_up, axis, [(d, (d + 1) % ways) for d in range(ways)])
+        full = lax.dynamic_update_slice_in_dim(full, going_up, (here - far) % ways * step, axis=dim)
+        if 2 * far < ways:
+            going_down = lax.ppermute(going_down, axis, [(d, (d - 1) % ways) for d in range(ways)])
+            full = lax.dynamic_update_slice_in_dim(
+                full, going_down, (here + far) % ways * step, axis=dim
+            )
+    return full
 
 
 def rms_norm(values, gain):
@@ -80,7 +98,7 @@
     query_full, key_full, value_full, out_full = (
         lax.all_gather(query_weight, ("fsdp", "ctx"), axis=0, tiled=True),
         lax.all_gather(key_weight, ("fsdp", "ctx"), axis=0, tiled=True),
-        lax.all_gather(value_weight, ("fsdp", "ctx"), axis=0, tiled=True),
+        gather_around(value_weight, ("fsdp", "ctx"), 0),
         lax.all_gather(out_weight, ("fsdp", "ctx"), axis=0, tiled=True),
     )
     queries_raw = jnp.dot(rows_one, query_full, preferred_element_type=jnp.float32).reshape(

time: 1160 us -> 1150 us (level)
  waiting for transfers between devices: 750 us -> 726 us
  starting transfers between devices: 2.17 us -> 17.8 us
    unnamed x23, waiting for transfers between devices: 32 us -> 2.73 us
    ppermute x0 -> x7, starting transfers between devices: none -> 15.6 us  [the longest x3 12.5 us: gather_around(): lax.ppermute(going_down, axis, [(d, (d - 1) % ways) for d in range(ways)])]
  transfers between devices with their start and end apart: 22 -> 29, of which waited for: 19 -> 21; matrix products, arithmetic and copies ran while one was open for 11% -> 11% of each run, Pallas kernels for 0% -> 0%
where the time goes in v1:
time: 1150 us; the launch traced here: 1140 us
  waiting for transfers between devices  726 us (63%)
  blocking collectives  169 us (15%)
  matrix products  123 us (11%)
  other arithmetic  56.4 us (5%)
  local copies, waits for them, and re-layouts  33.4 us (3%)
  starting transfers between devices  17.8 us (2%)
  between operations  17 us (1%)
    reduce_scatter x4, waiting for transfers between devices, scatter_rows(): return lax.psum_scatter(values, 'tp', scatter_dimension=1, tiled=True)  137 us
    reduce_scatter x1, waiting for transfers between devices, shards(): lax.psum_scatter(gate_local.astype(jnp.bfloat16), ('fsdp', 'ctx'), scatte...  68.3 us
    reduce_scatter x1, waiting for transfers between devices, shards(): lax.psum_scatter(up_local.astype(jnp.bfloat16), ('fsdp', 'ctx'), scatter_...  65.8 us
    reduce_scatter x1, waiting for transfers between devices, shards(): lax.psum_scatter(query_local.astype(jnp.bfloat16), ('fsdp', 'ctx'), scatt...  63.7 us
    reduce_scatter x1, waiting for transfers between devices, shards(): lax.psum_scatter(key_local.astype(jnp.bfloat16), ('fsdp', 'ctx'), scatter...  63.3 us
    reduce_scatter x1, waiting for transfers between devices, shards(): lax.psum_scatter(value_local.astype(jnp.bfloat16), ('fsdp', 'ctx'), scatt...  63 us
    reduce_scatter x1, waiting for transfers between devices, shards(): lax.psum_scatter(out_local.astype(jnp.bfloat16), ('fsdp', 'ctx'), scatter...  62.3 us
    all_gather x4, waiting for transfers between devices, gather_rows(): return lax.all_gather(values, 'tp', axis=1, tiled=True)  61.4 us
  transfers between devices with their start and end apart: 29, of which 21 were waited for; matrix products, arithmetic and copies ran while one was open for 11% of the time, Pallas kernels for 0%

profile of v1, /device:TPU:0, one launch (start us, length us, event | category | flops | bytes accessed | tf_op | source)
XLA Modules:
  0.0 1142.2 jit_solution(18428725759862909233)
XLA Ops:
  21.7 31.9 %all_gather.47 = bf16[1024,256]{1,0:T(8,128)(2,1)S(1)} all-gather(bf16[128,256]{1,0:T(8,128)(2,1)} %param.18), channel_id=1, replica_groups=mesh['fsdp'=4,'ctx'=2,'tp'=4] {'fsdp','ctx'}, dimensions={0}, use_global_device_ids=true | all-gather | bytes 589824 | tf_op jit(solution)/shard_map/all_gather | solution.py:99
  53.6 31.7 %all_gather.48 = bf16[1024,256]{1,0:T(8,128)(2,1)S(1)} all-gather(bf16[128,256]{1,0:T(8,128)(2,1)} %param.19), channel_id=1, replica_groups=mesh['fsdp'=4,'ctx'=2,'tp'=4] {'fsdp','ctx'}, dimensions={0}, use_global_device_ids=true | all-gather | bytes 589824 | tf_op jit(solution)/shard_map/all_gather | solution.py:100
  85.3 31.8 %all_gather.50 = bf16[1024,256]{1,0:T(8,128)(2,1)S(1)} all-gather(bf16[128,256]{1,0:T(8,128)(2,1)} %param.21), channel_id=1, replica_groups=mesh['fsdp'=4,'ctx'=2,'tp'=4] {'fsdp','ctx'}, dimensions={0}, use_global_device_ids=true | all-gather | bytes 589824 | tf_op jit(solution)/shard_map/all_gather | solution.py:102
  150.4 10.7 all-gather.12.cloned.1.call-done
  167.5 17.1 %all-gather.14.cloned.1.call-done = bf16[2,1024,256]{1,2,0:T(8,128)(2,1)} async-done(((bf16[2,512,256]{1,2,0:T(8,128)(2,1)}), bf16[2,1024,256]{1,2,0:T(8,128)(2,1)}) %all-gather.14.cloned.1.call-update) | async-done | bytes 1048592 | tf_op jit(solution)/shard_map/all_gather | solution.py:118
  211.8 43.6 %reduce-scatter.16.cloned.1.call-done = f32[2,128,1024]{2,1,0:T(8,128)} async-done(((f32[2,512,1024]{2,1,0:T(8,128)}), f32[2,128,1024]{2,1,0:T(8,128)}) %reduce-scatter.16.cloned.1.call-update) | async-done | bytes 1048592 | tf_op jit(solution)/shard_map/reduce_scatter | solution.py:57
  262.9 23.0 %all-gather.16.cloned.1.call-done = bf16[2,512,1024]{2,1,0:T(8,128)(2,1)} async-done(((bf16[2,128,1024]{2,1,0:T(8,128)(2,1)}), bf16[2,512,1024]{2,1,0:T(8,128)(2,1)}) %all-gather.16.cloned.1.call-update) | async-done | bytes 2097168 | tf_op jit(solution)/shard_map/all_gather | solution.py:53
  292.5 45.0 %all-gather.18.cloned.1.call-done = bf16[1024,1024]{1,0:T(8,128)(2,1)} async-done(((bf16[128,1024]{1,0:T(8,128)(2,1)}), bf16[1024,1024]{1,0:T(8,128)(2,1)}) %all-gather.18.cloned.1.call-update) | async-done | bytes 2097168 | tf_op jit(solution)/shard_map/all_gather | solution.py:166
  344.1 16.1 %all-gather.24.cloned.1.call-done = bf16[2,512,1024]{2,1,0:T(8,128)(2,1)} async-done(((bf16[2,128,1024]{2,1,0:T(8,128)(2,1)}), bf16[2,512,1024]{2,1,0:T(8,128)(2,1)}) %all-gather.24.cloned.1.call-update) | async-done | bytes 2097168 | tf_op jit(solution)/shard_map/all_gather | solution.py:53
  360.1 51.7 %all-gather.22.cloned.1.call-done = bf16[1024,1024]{1,0:T(8,128)(2,1)} async-done(((bf16[128,1024]{1,0:T(8,128)(2,1)}), bf16[1024,1024]{1,0:T(8,128)(2,1)}) %all-gather.22.cloned.1.call-update) | async-done | bytes 2097168 | tf_op jit(solution)/shard_map/all_gather | solution.py:168
  411.9 9.9 multiply_convert_fusion.2
  429.3 43.1 %reduce-scatter.20.cloned.1.call-done = f32[2,128,1024]{2,1,0:T(8,128)} async-done(((f32[2,512,1024]{2,1,0:T(8,128)}), f32[2,128,1024]{2,1,0:T(8,128)}) %reduce-scatter.20.cloned.1.call-update) | async-done | bytes 1048592 | tf_op jit(solution)/shard_map/reduce_scatter | solution.py:57
  477.2 22.2 %all-gather.26.cloned.1.call-done = bf16[2,512,1024]{2,1,0:T(8,128)(2,1)} async-done(((bf16[2,128,1024]{2,1,0:T(8,128)(2,1)}), bf16[2,512,1024]{2,1,0:T(8,128)(2,1)}) %all-gather.26.cloned.1.call-update) | async-done | bytes 2097168 | tf_op jit(solution)/shard_map/all_gather | solution.py:53
  507.7 7.3 multiply_reduce_fusion.1
  523.8 8.7 fusion
  590.9 33.5 %all_gather.57 = bf16[1024,256]{1,0:T(8,128)(2,1)} all-gather(bf16[128,256]{1,0:T(8,128)(2,1)S(1)} %copy-done.31), channel_id=1, replica_groups=mesh['fsdp'=4,'ctx'=2,'tp'=4] {'fsdp','ctx'}, dimensions={0}, use_global_device_ids=true | all-gather | bytes 589824 | tf_op jit(solution)/shard_map/all_gather | solution.py:180
  643.2 65.8 %reduce-scatter.38.cloned.1.call-done = bf16[128,1024]{1,0:T(8,128)(2,1)} async-done(((bf16[1024,1024]{1,0:T(8,128)(2,1)}), bf16[128,1024]{1,0:T(8,128)(2,1)}) %reduce-scatter.38.cloned.1.call-update) | async-done | bytes 262160 | tf_op jit(solution)/shard_map/reduce_scatter | solution.py:323
  710.8 68.3 %reduce-scatter.36.cloned.1.call-done = bf16[128,1024]{1,0:T(8,128)(2,1)} async-done(((bf16[1024,1024]{1,0:T(8,128)(2,1)}), bf16[128,1024]{1,0:T(8,128)(2,1)}) %reduce-scatter.36.cloned.1.call-update) | async-done | bytes 262160 | tf_op jit(solution)/shard_map/reduce_scatter | solution.py:320
  781.1 62.3 %reduce-scatter.34.cloned.1.call-done = bf16[128,256]{1,0:T(8,128)(2,1)} async-done(((bf16[1024,256]{1,0:T(8,128)(2,1)}), bf16[128,256]{1,0:T(8,128)(2,1)}) %reduce-scatter.34.cloned.1.call-update) | async-done | bytes 65552 | tf_op jit(solution)/shard_map/reduce_scatter | solution.py:315
  844.9 63.0 %reduce-scatter.32.cloned.1.call-done = bf16[128,256]{1,0:T(8,128)(2,1)} async-done(((bf16[1024,256]{1,0:T(8,128)(2,1)}), bf16[128,256]{1,0:T(8,128)(2,1)}) %reduce-scatter.32.cloned.1.call-update) | async-done | bytes 65552 | tf_op jit(solution)/shard_map/reduce_scatter | solution.py:312
  909.4 63.3 %reduce-scatter.30.cloned.1.call-done = bf16[128,256]{1,0:T(8,128)(2,1)} async-done(((bf16[1024,256]{1,0:T(8,128)(2,1)}), bf16[128,256]{1,0:T(8,128)(2,1)}) %reduce-scatter.30.cloned.1.call-update) | async-done | bytes 65552 | tf_op jit(solution)/shard_map/reduce_scatter | solution.py:309
  974.2 63.7 %reduce-scatter.28.cloned.1.call-done = bf16[128,256]{1,0:T(8,128)(2,1)} async-done(((bf16[1024,256]{1,0:T(8,128)(2,1)}), bf16[128,256]{1,0:T(8,128)(2,1)}) %reduce-scatter.28.cloned.1.call-update) | async-done | bytes 65552 | tf_op jit(solution)/shard_map/reduce_scatter | solution.py:306
  1039.4 44.4 %reduce-scatter.26.cloned.1.call-done = f32[2,128,1024]{2,1,0:T(8,128)} async-done(((f32[2,512,1024]{2,1,0:T(8,128)}), f32[2,128,1024]{2,1,0:T(8,128)}) %reduce-scatter.26.cloned.1.call-update) | async-done | bytes 1048592 | tf_op jit(solution)/shard_map/reduce_scatter | solution.py:57
  1085.4 39.8 %all-reduce.4 = (f32[1024]{0:T(1024)}, f32[1024]{0:T(1024)}, f32[2,16]{1,0:T(2,128)S(1)}) all-reduce(f32[1024]{0:T(1024)S(1)} %get-tuple-element.206, f32[1024]{0:T(1024)S(1)} %copy-done.45, f32[2,16]{1,0:T(2,128)S(1)} %dynamic_update_slice.50), channel_id=1, replica_groups=mesh['fsdp'=4,'ctx'=2,'tp'=4] {'fsdp','ctx','tp'}, use_global_device_ids=true, to_apply=%region_17.18 | all-reduce | flops 2080 | bytes 16640 | tf_op jit(solution)/shard_map/psum | solution.py:334
  (310 shorter events, 227.1 us)
Async XLA Ops:
  8.0 131.1 %all-gather.10.cloned.1.call-start = ((), (), s32[]{:S(2)}) async-start(), calls=%async_computation.13 | async-start | bytes 2621440 | tf_op jit(solution)/shard_map/all_gather | solution.py:53
  13.2 148.0 %all-gather.12.cloned.1.call-start = ((), (), s32[]{:S(2)}) async-start(), calls=%async_computation.14 | async-start | bytes 1572864 | tf_op jit(solution)/shard_map/all_gather | solution.py:119
  13.2 104.9 %collective-permute-start = (bf16[128,256]{1,0:T(8,128)(2,1)}, bf16[128,256]{1,0:T(8,128)(2,1)S(1)}, u32[]{:S(2)}, u32[]{:S(2)}) collective-permute-start(bf16[128,256]{1,0:T(8,128)(2,1)} %param.20), channel_id=1, source_target_pairs={{0,4},{4,8},{8,12},{12,16},{16,20},{20,24},{24,28},{28,0},{1,5},{5... | collective-permute-start | bytes 196616 | tf_op jit(solution)/shard_map/ppermute | solution.py:20
  16.2 102.0 %collective-permute-start.1 = (bf16[128,256]{1,0:T(8,128)(2,1)}, bf16[128,256]{1,0:T(8,128)(2,1)S(1)}, u32[]{:S(2)}, u32[]{:S(2)}) collective-permute-start(bf16[128,256]{1,0:T(8,128)(2,1)} %param.20), channel_id=1, source_target_pairs={{0,28},{4,0},{8,4},{12,8},{16,12},{20,16},{24,20},{28,24},{1,29},{... | collective-permute-start | bytes 196616 | tf_op jit(solution)/shard_map/ppermute | solution.py:23
  142.2 42.4 %all-gather.14.cloned.1.call-start = ((), (), s32[]{:S(2)}) async-start(), calls=%async_computation.15 | async-start | bytes 1572864 | tf_op jit(solution)/shard_map/all_gather | solution.py:118
  147.4 108.0 %reduce-scatter.16.cloned.1.call-start = ((), (), s32[]{:S(2)}) async-start(), calls=%async_computation.16 | async-start | bytes 5242880 | tf_op jit(solution)/shard_map/reduce_scatter | solution.py:57
  210.7 52.2 %all-gather.20.cloned.1.call-start = ((), (), s32[]{:S(2)}) async-start(), calls=%async_computation.19 | async-start | bytes 2359296 | tf_op jit(solution)/shard_map/all_gather | solution.py:167
  211.3 74.6 %all-gather.16.cloned.1.call-start = ((), (), s32[]{:S(2)}) async-start(), calls=%async_computation.17 | async-start | bytes 2621440 | tf_op jit(solution)/shard_map/all_gather | solution.py:53
  257.9 79.7 %all-gather.18.cloned.1.call-start = ((), (), s32[]{:S(2)}) async-start(), calls=%async_computation.18 | async-start | bytes 2359296 | tf_op jit(solution)/shard_map/all_gather | solution.py:166
  258.4 101.7 %all-gather.24.cloned.1.call-start = ((), (), s32[]{:S(2)}) async-start(), calls=%async_computation.22 | async-start | bytes 2621440 | tf_op jit(solution)/shard_map/all_gather | solution.py:53
  259.2 152.7 %all-gather.22.cloned.1.call-start = ((), (), s32[]{:S(2)}) async-start(), calls=%async_computation.20 | async-start | bytes 2359296 | tf_op jit(solution)/shard_map/all_gather | solution.py:168
  259.9 212.5 %reduce-scatter.20.cloned.1.call-start = ((), (), s32[]{:S(2)}) async-start(), calls=%async_computation.23 | async-start | bytes 5242880 | tf_op jit(solution)/shard_map/reduce_scatter | solution.py:57
  429.3 70.1 %all-gather.26.cloned.1.call-start = ((), (), s32[]{:S(2)}) async-start(), calls=%async_computation.24 | async-start | bytes 2621440 | tf_op jit(solution)/shard_map/all_gather | solution.py:53
  476.9 98.7 %reduce-scatter.24.cloned.1.call-start = ((), (), s32[]{:S(2)}) async-start(), calls=%async_computation.26 | async-start | bytes 1572864 | tf_op jit(solution)/shard_map/reduce_scatter | solution.py:270
  523.7 60.0 %reduce-scatter.22.cloned.1.call-start = ((), (), s32[]{:S(2)}) async-start(), calls=%async_computation.25 | async-start | bytes 1572864 | tf_op jit(solution)/shard_map/reduce_scatter | solution.py:267
  545.3 95.8 %reduce-scatter.40.cloned.1.call-start = ((), (), s32[]{:S(2)}) async-start(), calls=%async_computation.34 | async-start | bytes 2359296
  555.7 153.3 %reduce-scatter.38.cloned.1.call-start = ((), (), s32[]{:S(2)}) async-start(), calls=%async_computation.33 | async-start | bytes 2359296 | tf_op jit(solution)/shard_map/reduce_scatter | solution.py:323
  561.7 217.4 %reduce-scatter.36.cloned.1.call-start = ((), (), s32[]{:S(2)}) async-start(), calls=%async_computation.32 | async-start | bytes 2359296 | tf_op jit(solution)/shard_map/reduce_scatter | solution.py:320
  567.7 275.7 %reduce-scatter.34.cloned.1.call-start = ((), (), s32[]{:S(2)}) async-start(), calls=%async_computation.31 | async-start | bytes 589824 | tf_op jit(solution)/shard_map/reduce_scatter | solution.py:315
  571.0 337.0 %reduce-scatter.32.cloned.1.call-start = ((), (), s32[]{:S(2)}) async-start(), calls=%async_computation.30 | async-start | bytes 589824 | tf_op jit(solution)/shard_map/reduce_scatter | solution.py:312
  578.8 393.9 %reduce-scatter.30.cloned.1.call-start = ((), (), s32[]{:S(2)}) async-start(), calls=%async_computation.29 | async-start | bytes 589824 | tf_op jit(solution)/shard_map/reduce_scatter | solution.py:309
  590.8 447.1 %reduce-scatter.28.cloned.1.call-start = ((), (), s32[]{:S(2)}) async-start(), calls=%async_computation.28 | async-start | bytes 589824 | tf_op jit(solution)/shard_map/reduce_scatter | solution.py:306
  628.7 455.2 %reduce-scatter.26.cloned.1.call-start = ((), (), s32[]{:S(2)}) async-start(), calls=%async_computation.27 | async-start | bytes 5242880 | tf_op jit(solution)/shard_map/reduce_scatter | solution.py:57
  634.2 497.4 %reduce-scatter.18.cloned.1.call-start = ((), (), s32[]{:S(2)}) async-start(), calls=%async_computation.21 | async-start | bytes 5242880 | tf_op jit(solution)/shard_map/reduce_scatter | solution.py:57
  (74 other events, 5602.9 us)
Sparse Core Ops, SparseCore 0:
  13.3 25.2 all-gather.9
  142.4 18.7 all-gather.11
  163.3 21.2 all-gather.13
  210.8 44.5 reduce-scatter.15
  429.4 42.9 reduce-scatter.19
  523.8 20.3 reduce-scatter.23
  546.5 20.2 reduce-scatter.21
  570.3 68.4 reduce-scatter.39
  642.4 66.5 reduce-scatter.37
  712.4 66.6 reduce-scatter.35
  782.4 60.9 reduce-scatter.33
  846.9 60.9 reduce-scatter.31
  911.8 60.8 reduce-scatter.29
  976.8 61.0 reduce-scatter.27
  1040.3 43.4 reduce-scatter.25
  1086.3 45.2 reduce-scatter.17
Sparse Core Ops, SparseCore 1:
  213.5 49.3 all-gather.19
  265.0 20.9 all-gather.15
  288.2 49.3 all-gather.17
  339.2 20.9 all-gather.23
  362.5 49.3 all-gather.21
  477.0 22.4 all-gather.25
